TPU v7x, 32 devices: a whole 2x2x4 slice. The times are simulated.
32 devices in a mesh: seq: 8 (over z, y), head: 4 (over x, core).
Axes of the slice: x: 2, y: 2, z: 4, core: 2. Of those that a mesh axis runs over, the one named last changes fastest.
Arguments:
- queries: bfloat16 [1024, 8, 128], P('seq', 'head'), may hold values from -16 to 16
- values: bfloat16 [1024, 8, 128], P('seq', 'head'), may hold values from -6 to 6
- codes: int32 [8, 1024], P('head', 'seq'), may hold values from 0 to 511, as said below
- codebook: bfloat16 [8, 512, 128], P('head'), may hold values from -0.5 to 0.5
- out_weight: bfloat16 [1024, 2048], P('head'), may hold values from -0.1875 to 0.1875
- grad_out: bfloat16 [1024, 2048], P('seq', 'head'), may hold values from -6 to 6
Outputs:
- grad_queries: bfloat16 [1024, 8, 128], P('seq', 'head')
- grad_values: bfloat16 [1024, 8, 128], P('seq', 'head')
- grad_codebook: float32 [8, 512, 128], P('head')
- grad_weight: bfloat16 [1024, 2048], P('head')
Inputs may be any that keep to these rules, and one draw needn't show every extreme that they name: `codes`: each head's key codeword at each token; both 0 and 511 occur.
All inputs are finite; a program needn't handle non-finite values.
Results may differ from a plain program's by a relative error of at most 0.0065.
Values may be sent and summed in bfloat16 or wider, within the bound.
No kernel may reach another device: no remote copies, remote signals or barrier semaphores. Data moves between devices by JAX's collectives and lax.ppermute only.
A program may use at most 256 MiB of HBM per device.

v0:
```python
import jax
import jax.numpy as jnp
from jax import lax
from jax.sharding import PartitionSpec as P

BLOCK = 128


def entering(value, axis, join, neutral, backward):
    count, mine = (lax.axis_size(axis), lax.axis_index(axis))
    pieces = jax.tree.map(lambda part: lax.all_gather(part, axis), value)
    if backward:
        pieces = jax.tree.map(lambda part: part[::-1], pieces)
        mine = count - 1 - mine
    so_far = jax.tree.map(
        lambda part, zero: jnp.full_like(part, 0) + jnp.asarray(zero, part.dtype), value, neutral
    )

    def turn(position, so_far):
        longer = join(so_far, jax.tree.map(lambda part: part[position], pieces))
        return jax.tree.map(lambda new, old: jnp.where(position < mine, new, old), longer, so_far)

    return lax.fori_loop(0, count - 1, turn, so_far)


def inner_rows(left_side, right_side):
    return lax.dot_general(
        left_side, right_side, (((0,), (0,)), ((), ())), preferred_element_type=jnp.float32
    )


def block_core(query_rows, code_rows, value_rows, grad_rows, cache_sum, cache_count, codebook_head):
    key_rows = jnp.take(codebook_head, code_rows, axis=0)
    contract_last = (((1,), (1,)), ((), ()))
    local_score = lax.dot_general(
        query_rows, key_rows, contract_last, preferred_element_type=jnp.float32
    )
    code_score = lax.dot_general(
        query_rows, codebook_head, contract_last, preferred_element_type=jnp.float32
    )
    length = query_rows.shape[0]
    row_index = lax.broadcasted_iota(jnp.int32, (length, length), 0)
    col_index = lax.broadcasted_iota(jnp.int32, (length, length), 1)
    causal = col_index <= row_index
    top_score = jnp.maximum(
        jnp.max(jnp.where(causal, local_score, -jnp.inf), axis=1), jnp.max(code_score, axis=1)
    )
    weights = jnp.where(causal, jnp.exp(local_score - top_score[:, None]), jnp.float32(0.0))
    cache_weight = jnp.exp(code_score - top_score[:, None])
    denominator = jnp.sum(weights, axis=1) + jnp.sum(cache_weight * cache_count[None, :], axis=1)
    cache_round = cache_sum.astype(jnp.bfloat16)
    numerator = jnp.dot(
        weights.astype(jnp.bfloat16), value_rows, preferred_element_type=jnp.float32
    )
    numerator = numerator + jnp.dot(
        cache_weight.astype(jnp.bfloat16), cache_round, preferred_element_type=jnp.float32
    )
    attended = numerator / denominator[:, None]
    row_delta = jnp.sum(grad_rows.astype(jnp.float32) * attended, axis=1)
    local_grad = lax.dot_general(
        grad_rows, value_rows, contract_last, preferred_element_type=jnp.float32
    )
    cache_grad = lax.dot_general(
        grad_rows, cache_round, contract_last, preferred_element_type=jnp.float32
    )
    grad_local = (weights * (local_grad - row_delta[:, None]) / denominator[:, None]).astype(
        jnp.bfloat16
    )
    grad_cache = (
        cache_weight
        * (cache_grad - row_delta[:, None] * cache_count[None, :])
        / denominator[:, None]
    ).astype(jnp.bfloat16)
    grad_query = jnp.dot(grad_local, key_rows, preferred_element_type=jnp.float32)
    grad_query = (
        grad_query + jnp.dot(grad_cache, codebook_head, preferred_element_type=jnp.float32)
    ).astype(jnp.bfloat16)
    grad_key = inner_rows(grad_local, query_rows)
    key_high = grad_key.astype(jnp.bfloat16)
    key_low = (grad_key - key_high.astype(jnp.float32)).astype(jnp.bfloat16)
    selector = (
        code_rows[:, None] == jnp.arange(codebook_head.shape[0], dtype=jnp.int32)[None, :]
    ).astype(jnp.bfloat16)
    grad_book = inner_rows(selector, key_high) + inner_rows(selector, key_low)
    grad_book = grad_book + inner_rows(grad_cache, query_rows)
    local_share = (weights / denominator[:, None]).astype(jnp.bfloat16)
    cache_share = (cache_weight / denominator[:, None]).astype(jnp.bfloat16)
    grad_value = inner_rows(local_share, grad_rows)
    grad_sum = inner_rows(cache_share, grad_rows)
    return (grad_query, grad_value, grad_sum, grad_book, attended.astype(jnp.bfloat16))


def exclusive_forward(stacked):
    summed = jnp.cumsum(stacked, axis=1)
    return jnp.concatenate([jnp.zeros_like(stacked), summed[:, :-1]], axis=1)


def exclusive_backward(stacked):
    summed = jnp.flip(jnp.cumsum(jnp.flip(stacked, axis=1), axis=1), axis=1)
    return jnp.concatenate([summed[:, 1:], jnp.zeros_like(stacked)], axis=1)


def on_device(queries, values, codes, codebook, out_weight, grad_out):
    tok_here, heads_here, head_width = queries.shape
    code_total = codebook.shape[1]
    blocks = tok_here // BLOCK
    full_grad = lax.all_gather(grad_out, "head", axis=1, tiled=True)
    grad_flat = lax.dot_general(
        full_grad, out_weight, (((1,), (1,)), ((), ())), preferred_element_type=jnp.float32
    ).astype(jnp.bfloat16)
    grad_heads = grad_flat.reshape(tok_here, heads_here, head_width)

    def to_blocks(array):
        return jnp.moveaxis(array.reshape(blocks, BLOCK, heads_here, head_width), 2, 0)

    def from_blocks(array):
        return jnp.moveaxis(array, 0, 2).reshape(tok_here, heads_here, head_width)

    def flatten(array):
        return array.reshape((heads_here * blocks,) + array.shape[2:])

    def unflatten(array):
        return array.reshape((heads_here, blocks) + array.shape[1:])

    code_blocks = codes.reshape(heads_here, blocks, BLOCK)
    query_blocks = to_blocks(queries)
    value_blocks = to_blocks(values)
    grad_blocks = to_blocks(grad_heads)
    selector = (code_blocks[..., None] == jnp.arange(code_total, dtype=jnp.int32)).astype(
        jnp.bfloat16
    )
    block_sums = jnp.einsum(
        "hnbc,hnbd->hncd", selector, value_blocks, preferred_element_type=jnp.float32
    )
    block_counts = jnp.sum(selector, axis=2, dtype=jnp.float32)
    device_parts = (jnp.sum(block_sums, axis=1), jnp.sum(block_counts, axis=1))
    earlier = entering(
        device_parts,
        "seq",
        lambda first_part, second_part: (
            first_part[0] + second_part[0],
            first_part[1] + second_part[1],
        ),
        (jnp.zeros_like(device_parts[0]), jnp.zeros_like(device_parts[1])),
        False,
    )
    cache_sums = earlier[0][:, None] + exclusive_forward(block_sums)
    cache_counts = earlier[1][:, None] + exclusive_forward(block_counts)
    books = jnp.repeat(codebook, blocks, axis=0)
    results = lax.map(
        lambda block_items: block_core(*block_items),
        (
            flatten(query_blocks),
            flatten(code_blocks),
            flatten(value_blocks),
            flatten(grad_blocks),
            flatten(cache_sums),
            flatten(cache_counts),
            books,
        ),
    )
    grad_query = unflatten(results[0])
    grad_value = unflatten(results[1])
    grad_sums = unflatten(results[2])
    grad_books = unflatten(results[3])
    attended = unflatten(results[4])
    device_grad = jnp.sum(grad_sums, axis=1)
    later_grad = entering(
        device_grad,
        "seq",
        lambda first_part, second_part: first_part + second_part,
        jnp.zeros_like(device_grad),
        True,
    )
    carried = later_grad[:, None] + exclusive_backward(grad_sums)
    picked = jax.vmap(jax.vmap(lambda table_rows, indices: jnp.take(table_rows, indices, axis=0)))(
        carried, code_blocks
    )
    grad_values = (grad_value + picked).astype(jnp.bfloat16)
    book_here = jnp.sum(grad_books, axis=1)
    attended_flat = from_blocks(attended).reshape(tok_here, heads_here * head_width)
    weight_term = inner_rows(attended_flat, full_grad)
    summed_weight, summed_book = lax.psum((weight_term, book_here), "seq")
    grad_weight = summed_weight.astype(jnp.bfloat16)
    return (from_blocks(grad_query), from_blocks(grad_values), summed_book, grad_weight)


def solution(mesh):
    return jax.shard_map(
        on_device,
        mesh=mesh,
        in_specs=(
            P("seq", "head", None),
            P("seq", "head", None),
            P("head", "seq"),
            P("head", None, None),
            P("head", None),
            P("seq", "head"),
        ),
        out_specs=(
            P("seq", "head", None),
            P("seq", "head", None),
            P("head", None, None),
            P("head", None),
        ),
        check_vma=False,
    )
```

profile of v0, /device:TPU:0, one launch (start us, length us, event | category | flops | bytes accessed | tf_op | source)
XLA Modules:
  0.0 321.5 jit_solution(7390471878237787274)
XLA Ops:
  7.2 2.0 fusion.71
  10.2 8.9 %all_gather.21 = bf16[128,2048]{1,0:T(8,128)(2,1)S(1)} all-gather(bf16[128,512]{1,0:T(8,128)(2,1)} %param.17), channel_id=1, replica_groups=mesh['seq'=8,'head'=4] {'head'}, dimensions={1}, use_global_device_ids=true | all-gather | bytes 655360 | tf_op jit(solution)/shard_map/all_gather | solution.py:107
  21.3 31.5 %all-gather.3 = f32[8,2,512]{2,1,0:T(2,128)S(1)} all-gather(f32[1,2,512]{2,1,0:T(2,128)S(1)} %bitcast.203), channel_id=3, replica_groups=mesh['seq'=8,'head'=4] {'seq'}, dimensions={0}, use_global_device_ids=true | all-gather | bytes 36864 | tf_op jit(solution)/shard_map/all_gather | solution.py:11
  52.9 33.6 %all-gather.7.cloned.1.call-done = f32[16,512,128]{2,1,0:T(8,128)} async-done(((f32[2,512,128]{2,1,0:T(8,128)}), f32[16,512,128]{2,1,0:T(8,128)}) %all-gather.7.cloned.1.call-update) | async-done | bytes 4194320 | tf_op jit(solution)/shard_map/all_gather | solution.py:11
  86.4 8.7 %while.49 = (s32[]{:T(128)}, f32[2,512,128]{2,1,0:T(8,128)S(1)}, f32[2,512]{1,0:T(2,128)S(1)}, s32[]{:T(128)}, f32[8,2,512,128]{3,2,1,0:T(8,128)}, /*index=5*/f32[8,2,512]{2,1,0:T(2,128)S(1)}, s32[]{:T(128)}, s32[]{:T(128)}) while((s32[]{:T(128)}, f32[2,512,128]{2,1,0:T(8,128)S(1)}, f32[2,512]{1,0:T(2,128)S(1)}, s32[]{:T(128)}, ...), condition=%wide.region_2.0_spmd.clone, body=%wide.region_1.0_spmd.clone.sunk | while | flops 396292 | bytes 1585267 | solution.py:23
  86.4 1.2 add_select_fusion.6
  87.7 1.2 add_select_fusion.6
  95.2 14.3 %while.48 = (s32[]{:T(128)}, bf16[2,128,128]{2,1,0:T(8,128)(2,1)}, f32[2,128,128]{2,0,1:T(2,128)}, f32[2,512,128]{2,1,0:T(8,128)}, f32[2,512,128]{2,1,0:T(8,128)...) while((s32[]{:T(128)}, bf16[2,128,128]{2,1,0:T(8,128)(2,1)}, ...), condition=%wide.region_9.10_spmd, body=%wide.region_3.9_spmd.sunk | while | flops 161253120 | bytes 12096661 | solution.py:150
  99.9 1.4 dynamic_update_slice.31
  107.0 1.4 dynamic_update_slice.31
  110.0 2.6 fusion.86
  112.6 1.5 copy.53
  114.1 115.8 %all-reduce.4 = bf16[256,2048]{1,0:T(8,128)(2,1)} all-reduce(f32[256,2048]{1,0:T(8,128)} %fusion.86), channel_id=1, replica_groups=mesh['seq'=8,'head'=4] {'seq'}, use_global_device_ids=true, to_apply=%region_13.14 | all-reduce | flops 524288 | bytes 3145728 | tf_op jit(solution)/shard_map/psum | solution.py:183
  230.0 9.5 %all-gather.9.cloned.1.call-done = f32[16,512,128]{2,1,0:T(8,128)} async-done(((f32[2,512,128]{2,1,0:T(8,128)}), f32[16,512,128]{2,1,0:T(8,128)}) %all-gather.9.cloned.1.call-update) | async-done | bytes 4194320 | tf_op jit(solution)/shard_map/all_gather | solution.py:11
  239.5 4.5 %rev.3 = f32[8,2,512,128]{3,2,1,0:T(8,128)} reverse(f32[8,2,512,128]{3,2,1,0:T(8,128)} %bitcast.193), dimensions={0} | reverse | bytes 8388608 | tf_op jit(solution)/shard_map/rev | solution.py:13
  244.0 8.6 %while.50 = (s32[]{:T(128)}, f32[2,512,128]{2,1,0:T(8,128)S(1)}, s32[]{:T(128)}, f32[8,2,512,128]{3,2,1,0:T(8,128)}, s32[]{:T(128)}, /*index=5*/s32[]{:T(128)}) while((s32[]{:T(128)}, f32[2,512,128]{2,1,0:T(8,128)S(1)}, s32[]{:T(128)}, f32[8,2,512,128]{3,2,1,0:T(8,128)}, s32[]{:T(128)}, /*index=5*/s32[]{:T(128)}) %tuple.98), condition=%wide.region_11.12_spmd.clone, body=%wide.region_10.11_spmd.clone.sunk | while | flops 393220 | bytes 1572957 | solution.py:23
  244.0 1.2 add_select_fusion.8
  245.3 1.2 add_select_fusion.8
  246.5 1.2 add_select_fusion.8
  250.2 1.2 add_select_fusion.8
  251.4 1.2 add_select_fusion.8
  252.6 1.9 gather_fusion.1
  255.4 57.7 %all-reduce.3.cloned.1.call-done = f32[2,512,128]{2,1,0:T(8,128)} async-done(((f32[2,512,128]{2,1,0:T(8,128)}), f32[2,512,128]{2,1,0:T(8,128)}) %all-reduce.3.cloned.1.call-update) | async-done | bytes 524304 | tf_op jit(solution)/shard_map/psum | solution.py:183
  313.1 1.9 copy.97
  (134 shorter events, 24.2 us)
Async XLA Ops:
  7.2 11.9 %copy-start = (bf16[256,2048]{1,0:T(8,128)(2,1)S(1)}, bf16[256,2048]{1,0:T(8,128)(2,1)}, u32[]{:S(2)}) copy-start(bf16[256,2048]{1,0:T(8,128)(2,1)} %param.16) | copy-start | bytes 3145732
  7.2 79.2 %all-gather.7.cloned.1.call-start = ((), (), s32[]{:S(2)}) async-start(), calls=%async_computation.1 | async-start | bytes 4718592 | tf_op jit(solution)/shard_map/all_gather | solution.py:11
  9.2 230.3 %all-gather.9.cloned.1.call-start = ((), (), s32[]{:S(2)}) async-start(), calls=%async_computation.2 | async-start | bytes 4718592 | tf_op jit(solution)/shard_map/all_gather | solution.py:11
  86.4 8.8 %copy-start.1 = (bf16[2,512,128]{2,1,0:T(8,128)(2,1)S(1)}, bf16[2,512,128]{2,1,0:T(8,128)(2,1)}, u32[]{:S(2)}) copy-start(bf16[2,512,128]{2,1,0:T(8,128)(2,1)} %param.15) | copy-start | bytes 786436
  86.4 8.8 %copy-start.12 = (s32[2,128]{1,0:T(2,128)S(1)}, s32[2,128]{1,0:T(2,128)}, u32[]{:S(2)}) copy-start(s32[2,128]{1,0:T(2,128)} %param.14) | copy-start | bytes 3076
  95.3 4.6 %copy-start.5 = (f32[2,128,128]{2,0,1:T(2,128)S(1)}, f32[2,128,128]{2,0,1:T(2,128)}, u32[]{:S(2)}) copy-start(f32[2,128,128]{2,0,1:T(2,128)} %get-tuple-element.601) | copy-start | bytes 393220 | tf_op jit(solution)/shard_map/while
  95.3 6.3 %copy-start.8 = (bf16[2,128,128]{2,1,0:T(8,128)(2,1)S(1)}, bf16[2,128,128]{2,1,0:T(8,128)(2,1)}, u32[]{:S(2)}) copy-start(bf16[2,128,128]{2,1,0:T(8,128)(2,1)} %get-tuple-element.600) | copy-start | bytes 196612 | tf_op jit(solution)/shard_map/while
  95.3 6.5 %copy-start.10 = (bf16[2,128,128]{1,2,0:T(8,128)(2,1)S(1)}, bf16[2,128,128]{1,2,0:T(8,128)(2,1)}, u32[]{:S(2)}) copy-start(bf16[2,128,128]{1,2,0:T(8,128)(2,1)} %get-tuple-element.604) | copy-start | bytes 196612 | tf_op jit(solution)/shard_map/while
  96.1 2.7 copy-start.3
  99.1 0.8 copy-start.4
  101.3 0.7 copy-start.6
  101.8 0.6 copy-start.9
  101.8 0.6 copy-start.11
  102.4 4.6 %copy-start.5 = (f32[2,128,128]{2,0,1:T(2,128)S(1)}, f32[2,128,128]{2,0,1:T(2,128)}, u32[]{:S(2)}) copy-start(f32[2,128,128]{2,0,1:T(2,128)} %get-tuple-element.601) | copy-start | bytes 393220 | tf_op jit(solution)/shard_map/while
  102.4 6.3 %copy-start.8 = (bf16[2,128,128]{2,1,0:T(8,128)(2,1)S(1)}, bf16[2,128,128]{2,1,0:T(8,128)(2,1)}, u32[]{:S(2)}) copy-start(bf16[2,128,128]{2,1,0:T(8,128)(2,1)} %get-tuple-element.600) | copy-start | bytes 196612 | tf_op jit(solution)/shard_map/while
  102.4 6.5 %copy-start.10 = (bf16[2,128,128]{1,2,0:T(8,128)(2,1)S(1)}, bf16[2,128,128]{1,2,0:T(8,128)(2,1)}, u32[]{:S(2)}) copy-start(bf16[2,128,128]{1,2,0:T(8,128)(2,1)} %get-tuple-element.604) | copy-start | bytes 196612 | tf_op jit(solution)/shard_map/while
  103.2 2.7 copy-start.3
  106.2 0.8 copy-start.4
  108.5 0.7 copy-start.6
  108.9 0.6 copy-start.9
  109.0 0.6 copy-start.11
  109.6 120.3 %copy-start.2 = (f32[2,512,128]{2,1,0:T(8,128)}, f32[2,512,128]{2,1,0:T(8,128)S(1)}, u32[]{:S(2)}) copy-start(f32[2,512,128]{2,1,0:T(8,128)S(1)} %get-tuple-element.270) | copy-start | bytes 1572868
  109.6 203.5 %all-reduce.3.cloned.1.call-start = ((), (), s32[]{:S(2)}) async-start(), calls=%async_computation | async-start | bytes 1048576 | tf_op jit(solution)/shard_map/psum | solution.py:183
  244.0 10.6 %copy-start.7 = (f32[2,128,128]{2,0,1:T(2,128)S(1)}, f32[2,128,128]{2,0,1:T(2,128)}, u32[]{:S(2)}) copy-start(f32[2,128,128]{2,0,1:T(2,128)} %get-tuple-element.267) | copy-start | bytes 393220
Sparse Core Ops, SparseCore 0:
  10.7 75.6 all-gather.6
  109.7 129.6 all-gather.8
  242.9 70.1 all-reduce.2
where the time goes:
time: 323 us; the launch traced here: 322 us
  blocking collectives  156 us (48%)
  waiting for transfers between devices  101 us (31%)
  other arithmetic  19.4 us (6%)
  local copies, waits for them, and re-layouts  18.8 us (6%)
  between operations  13.9 us (4%)
  matrix products  11.5 us (4%)
    psum x1, blocking collectives, on_device(): summed_weight, summed_book = lax.psum((weight_term, book_here), 'seq')  116 us
    psum x1, waiting for transfers between devices, on_device(): summed_weight, summed_book = lax.psum((weight_term, book_here), 'seq')  57.7 us
    all_gather x2, waiting for transfers between devices, entering(): pieces = jax.tree.map(lambda part: lax.all_gather(part, axis), value)  43.1 us
    all_gather x1, blocking collectives, entering(): pieces = jax.tree.map(lambda part: lax.all_gather(part, axis), value)  31.5 us
    select_n x21, other arithmetic, turn(): jnp.where(position < mine, new, old)  17.1 us
    all_gather x1, blocking collectives, on_device(): full_grad = lax.all_gather(grad_out, 'head', axis=1, tiled=True)  8.86 us
  transfers between devices with their start and end apart: 3, of which 3 were waited for; matrix products, arithmetic and copies ran while one was open for 7% of the time, Pallas kernels for 0%

commit v1 on v0

--- a/solution.py
+++ b/solution.py
@@ -104,7 +104,10 @@
     tok_here, heads_here, head_width = queries.shape
     code_total = codebook.shape[1]
     blocks = tok_here // BLOCK
-    full_grad = lax.all_gather(grad_out, "head", axis=1, tiled=True)
+    size = lax.axis_size("head")
+    parts = jnp.stack([grad_out for _ in range(size)])
+    parts = lax.all_to_all(parts, "head", split_axis=0, concat_axis=0)
+    full_grad = jnp.concatenate(parts, axis=1)
     grad_flat = lax.dot_general(
         full_grad, out_weight, (((1,), (1,)), ((), ())), preferred_element_type=jnp.float32
     ).astype(jnp.bfloat16)

time: 323 us -> 323 us (level)
  blocking collectives: 156 us -> 150 us
  starting transfers between devices: 0.12 us -> 4.32 us
    all_gather x1 -> x0, blocking collectives: 8.86 us -> none  [on_device(): full_grad = lax.all_gather(grad_out, 'head', axis=1, tiled=True)]
    all_to_all x0 -> x1, starting transfers between devices: none -> 4.23 us  [on_device(): parts = lax.all_to_all(parts, 'head', split_axis=0, concat_axis=0)]
  transfers between devices with their start and end apart: 3 -> 4, of which waited for: 3 -> 3; matrix products, arithmetic and copies ran while one was open for 7% -> 8% of each run, Pallas kernels for 0% -> 0%
where the time goes in v1:
time: 323 us; the launch traced here: 321 us
  blocking collectives  150 us (46%)
  waiting for transfers between devices  101 us (31%)
  local copies, waits for them, and re-layouts  20.7 us (6%)
  other arithmetic  19.4 us (6%)
  between operations  13.9 us (4%)
  matrix products  11.5 us (4%)
  starting transfers between devices  4.32 us (1%)
    psum x1, blocking collectives, on_device(): summed_weight, summed_book = lax.psum((weight_term, book_here), 'seq')  118 us
    psum x1, waiting for transfers between devices, on_device(): summed_weight, summed_book = lax.psum((weight_term, book_here), 'seq')  57.5 us
    all_gather x2, waiting for transfers between devices, entering(): pieces = jax.tree.map(lambda part: lax.all_gather(part, axis), value)  43.1 us
    all_gather x1, blocking collectives, entering(): pieces = jax.tree.map(lambda part: lax.all_gather(part, axis), value)  32.3 us
    select_n x21, other arithmetic, turn(): jnp.where(position < mine, new, old)  17 us
  transfers between devices with their start and end apart: 4, of which 3 were waited for; matrix products, arithmetic and copies ran while one was open for 8% of the time, Pallas kernels for 0%

profile of v1, /device:TPU:0, one launch (start us, length us, event | category | flops | bytes accessed | tf_op | source)
XLA Modules:
  0.0 321.5 jit_solution(15033503761919717102)
XLA Ops:
  7.2 2.0 fusion.71
  11.1 4.2 %all-to-all-start = ((bf16[4,128,512]{1,2,0:T(8,128)(2,1)}), bf16[4,128,512]{1,2,0:T(8,128)(2,1)S(1)}, u32[]{:S(2)}, u32[]{:S(2)}) async-start(bf16[4,128,512]{1,2,0:T(8,128)(2,1)} %stack.2), calls=%async_computation | async-start | bytes 1048576 | tf_op jit(solution)/shard_map/all_to_all | solution.py:109
  17.9 32.3 %all-gather.3 = f32[8,2,512]{2,1,0:T(2,128)S(1)} all-gather(f32[1,2,512]{2,1,0:T(2,128)S(1)} %bitcast.208), channel_id=3, replica_groups=mesh['seq'=8,'head'=4] {'seq'}, dimensions={0}, use_global_device_ids=true | all-gather | bytes 36864 | tf_op jit(solution)/shard_map/all_gather | solution.py:11
  50.9 35.0 %all-gather.7.cloned.1.call-done = f32[16,512,128]{2,1,0:T(8,128)} async-done(((f32[2,512,128]{2,1,0:T(8,128)}), f32[16,512,128]{2,1,0:T(8,128)}) %all-gather.7.cloned.1.call-update) | async-done | bytes 4194320 | tf_op jit(solution)/shard_map/all_gather | solution.py:11
  85.9 8.7 %while.49 = (s32[]{:T(128)}, f32[2,512,128]{2,1,0:T(8,128)S(1)}, f32[2,512]{1,0:T(2,128)S(1)}, s32[]{:T(128)}, f32[8,2,512,128]{3,2,1,0:T(8,128)}, /*index=5*/f32[8,2,512]{2,1,0:T(2,128)S(1)}, s32[]{:T(128)}, s32[]{:T(128)}) while((s32[]{:T(128)}, f32[2,512,128]{2,1,0:T(8,128)S(1)}, f32[2,512]{1,0:T(2,128)S(1)}, s32[]{:T(128)}, ...), condition=%wide.region_2.0_spmd.clone, body=%wide.region_1.0_spmd.clone.sunk | while | flops 396292 | bytes 1585267 | solution.py:23
  85.9 1.2 add_select_fusion.6
  87.2 1.2 add_select_fusion.6
  89.7 1.2 add_select_fusion.6
  94.7 14.3 %while.48 = (s32[]{:T(128)}, bf16[2,128,128]{2,1,0:T(8,128)(2,1)}, f32[2,128,128]{2,0,1:T(2,128)}, f32[2,512,128]{2,1,0:T(8,128)}, f32[2,512,128]{2,1,0:T(8,128)...) while((s32[]{:T(128)}, bf16[2,128,128]{2,1,0:T(8,128)(2,1)}, ...), condition=%wide.region_9.10_spmd, body=%wide.region_3.9_spmd.sunk | while | flops 161253120 | bytes 12096661 | solution.py:153
  99.4 1.4 dynamic_update_slice.31
  106.5 1.4 dynamic_update_slice.31
  109.5 2.6 fusion.86
  112.1 1.5 copy.65
  113.6 118.0 %all-reduce.4 = bf16[256,2048]{1,0:T(8,128)(2,1)} all-reduce(f32[256,2048]{1,0:T(8,128)} %fusion.86), channel_id=1, replica_groups=mesh['seq'=8,'head'=4] {'seq'}, use_global_device_ids=true, to_apply=%region_13.14 | all-reduce | flops 524288 | bytes 3145728 | tf_op jit(solution)/shard_map/psum | solution.py:186
  231.6 8.1 %all-gather.9.cloned.1.call-done = f32[16,512,128]{2,1,0:T(8,128)} async-done(((f32[2,512,128]{2,1,0:T(8,128)}), f32[16,512,128]{2,1,0:T(8,128)}) %all-gather.9.cloned.1.call-update) | async-done | bytes 4194320 | tf_op jit(solution)/shard_map/all_gather | solution.py:11
  239.7 4.5 %rev.3 = f32[8,2,512,128]{3,2,1,0:T(8,128)} reverse(f32[8,2,512,128]{3,2,1,0:T(8,128)} %bitcast.198), dimensions={0} | reverse | bytes 8388608 | tf_op jit(solution)/shard_map/rev | solution.py:13
  244.2 8.6 %while.50 = (s32[]{:T(128)}, f32[2,512,128]{2,1,0:T(8,128)S(1)}, s32[]{:T(128)}, f32[8,2,512,128]{3,2,1,0:T(8,128)}, s32[]{:T(128)}, /*index=5*/s32[]{:T(128)}) while((s32[]{:T(128)}, f32[2,512,128]{2,1,0:T(8,128)S(1)}, s32[]{:T(128)}, f32[8,2,512,128]{3,2,1,0:T(8,128)}, s32[]{:T(128)}, /*index=5*/s32[]{:T(128)}) %tuple.99), condition=%wide.region_11.12_spmd.clone, body=%wide.region_10.11_spmd.clone.sunk | while | flops 393220 | bytes 1572957 | solution.py:23
  244.2 1.2 add_select_fusion.8
  245.4 1.2 add_select_fusion.8
  250.4 1.2 add_select_fusion.8
  251.6 1.2 add_select_fusion.8
  252.8 1.9 gather_fusion.1
  255.6 57.5 %all-reduce.3.cloned.1.call-done = f32[2,512,128]{2,1,0:T(8,128)} async-done(((f32[2,512,128]{2,1,0:T(8,128)}), f32[2,512,128]{2,1,0:T(8,128)}) %all-reduce.3.cloned.1.call-update) | async-done | bytes 524304 | tf_op jit(solution)/shard_map/psum | solution.py:186
  313.1 1.9 copy.109
  (137 shorter events, 26.0 us)
Async XLA Ops:
  7.2 43.1 %copy-start = (bf16[256,2048]{1,0:T(8,128)(2,1)S(1)}, bf16[256,2048]{1,0:T(8,128)(2,1)}, u32[]{:S(2)}) copy-start(bf16[256,2048]{1,0:T(8,128)(2,1)} %param.16) | copy-start | bytes 3145732
  7.2 78.7 %all-gather.7.cloned.1.call-start = ((), (), s32[]{:S(2)}) async-start(), calls=%async_computation.2 | async-start | bytes 4718592 | tf_op jit(solution)/shard_map/all_gather | solution.py:11
  11.1 39.1 %all-to-all-start = ((bf16[4,128,512]{1,2,0:T(8,128)(2,1)}), bf16[4,128,512]{1,2,0:T(8,128)(2,1)S(1)}, u32[]{:S(2)}, u32[]{:S(2)}) async-start(bf16[4,128,512]{1,2,0:T(8,128)(2,1)} %stack.2), calls=%async_computation | async-start | bytes 1048576 | tf_op jit(solution)/shard_map/all_to_all | solution.py:109
  15.3 224.3 %all-gather.9.cloned.1.call-start = ((), (), s32[]{:S(2)}) async-start(), calls=%async_computation.3 | async-start | bytes 4718592 | tf_op jit(solution)/shard_map/all_gather | solution.py:11
  85.9 8.8 %copy-start.1 = (bf16[2,512,128]{2,1,0:T(8,128)(2,1)S(1)}, bf16[2,512,128]{2,1,0:T(8,128)(2,1)}, u32[]{:S(2)}) copy-start(bf16[2,512,128]{2,1,0:T(8,128)(2,1)} %param.15) | copy-start | bytes 786436
  85.9 8.8 %copy-start.12 = (s32[2,128]{1,0:T(2,128)S(1)}, s32[2,128]{1,0:T(2,128)}, u32[]{:S(2)}) copy-start(s32[2,128]{1,0:T(2,128)} %param.14) | copy-start | bytes 3076
  94.7 4.6 %copy-start.5 = (f32[2,128,128]{2,0,1:T(2,128)S(1)}, f32[2,128,128]{2,0,1:T(2,128)}, u32[]{:S(2)}) copy-start(f32[2,128,128]{2,0,1:T(2,128)} %get-tuple-element.614) | copy-start | bytes 393220 | tf_op jit(solution)/shard_map/while
  94.7 6.3 %copy-start.8 = (bf16[2,128,128]{2,1,0:T(8,128)(2,1)S(1)}, bf16[2,128,128]{2,1,0:T(8,128)(2,1)}, u32[]{:S(2)}) copy-start(bf16[2,128,128]{2,1,0:T(8,128)(2,1)} %get-tuple-element.613) | copy-start | bytes 196612 | tf_op jit(solution)/shard_map/while
  94.7 6.5 %copy-start.10 = (bf16[2,128,128]{1,2,0:T(8,128)(2,1)S(1)}, bf16[2,128,128]{1,2,0:T(8,128)(2,1)}, u32[]{:S(2)}) copy-start(bf16[2,128,128]{1,2,0:T(8,128)(2,1)} %get-tuple-element.617) | copy-start | bytes 196612 | tf_op jit(solution)/shard_map/while
  95.5 2.7 copy-start.3
  98.6 0.8 copy-start.4
  100.8 0.6 copy-start.6
  101.2 0.6 copy-start.9
  101.3 0.6 copy-start.11
  101.9 4.6 %copy-start.5 = (f32[2,128,128]{2,0,1:T(2,128)S(1)}, f32[2,128,128]{2,0,1:T(2,128)}, u32[]{:S(2)}) copy-start(f32[2,128,128]{2,0,1:T(2,128)} %get-tuple-element.614) | copy-start | bytes 393220 | tf_op jit(solution)/shard_map/while
  101.9 6.3 %copy-start.8 = (bf16[2,128,128]{2,1,0:T(8,128)(2,1)S(1)}, bf16[2,128,128]{2,1,0:T(8,128)(2,1)}, u32[]{:S(2)}) copy-start(bf16[2,128,128]{2,1,0:T(8,128)(2,1)} %get-tuple-element.613) | copy-start | bytes 196612 | tf_op jit(solution)/shard_map/while
  101.9 6.5 %copy-start.10 = (bf16[2,128,128]{1,2,0:T(8,128)(2,1)S(1)}, bf16[2,128,128]{1,2,0:T(8,128)(2,1)}, u32[]{:S(2)}) copy-start(bf16[2,128,128]{1,2,0:T(8,128)(2,1)} %get-tuple-element.617) | copy-start | bytes 196612 | tf_op jit(solution)/shard_map/while
  102.7 2.7 copy-start.3
  105.7 0.8 copy-start.4
  107.9 0.6 copy-start.6
  108.4 0.6 copy-start.9
  109.0 122.5 %copy-start.2 = (f32[2,512,128]{2,1,0:T(8,128)}, f32[2,512,128]{2,1,0:T(8,128)S(1)}, u32[]{:S(2)}) copy-start(f32[2,512,128]{2,1,0:T(8,128)S(1)} %get-tuple-element.270) | copy-start | bytes 1572868
  109.1 204.0 %all-reduce.3.cloned.1.call-start = ((), (), s32[]{:S(2)}) async-start(), calls=%async_computation.1 | async-start | bytes 1048576 | tf_op jit(solution)/shard_map/psum | solution.py:186
  244.2 10.5 %copy-start.7 = (f32[2,128,128]{2,0,1:T(2,128)S(1)}, f32[2,128,128]{2,0,1:T(2,128)}, u32[]{:S(2)}) copy-start(f32[2,128,128]{2,0,1:T(2,128)} %get-tuple-element.267) | copy-start | bytes 393220
  (1 other events, 0.6 us)
Sparse Core Ops, SparseCore 0:
  10.1 75.7 all-gather.6
  109.2 130.4 all-gather.8
  243.1 69.9 all-reduce.2
